TPU v7x, 256 devices: a whole 4x4x8 slice. The times are simulated.
256 devices in a mesh: imp: 32 (over z, y_hi, core), cre: 8 (over x, y_lo).
Axes of the slice: x: 4, y: 4 (y_hi: 2, y_lo: 2; y = y_hi * 2 + y_lo), z: 8, core: 2. Of those that a mesh axis runs over, the one named last changes fastest.
Arguments:
- impressions: bfloat16 [32768, 256], P('imp'), may hold values from -24 to 24
- panels: bfloat16 [8, 2048, 256], P('cre', 'imp'), may hold values from -2 to 2
- block_lists: int32 [256, 16], P('imp'), may hold values from 0 to 127, as said below
- block_counts: int32 [256], P('imp'), may hold values from 1 to 16, as said below
- imp_weight: float32 [32768], P('imp'), may hold values from 0.2 to 5
- spend_goals: float32 [8, 2048], P('cre', 'imp'), may hold values from 0.2 to 5
- prices: float32 [8, 2048], P('cre', 'imp'), may hold values from -1 to 1
Outputs:
- final_prices: float32 [8, 2048], P('cre', 'imp')
- final_spend: float32 [8, 2048], P('cre', 'imp')
- log_norm: float32 [32768], P('imp')
Inputs may be any that keep to these rules, and one draw needn't show every extreme that they name: `block_lists`: each row lists 16 different block ids; only the first block_counts entries of a row are eligible for the 128 impressions of that tile, the others must be ignored. `block_counts`: some tile has 16 eligible blocks.
All inputs are finite; a program needn't handle non-finite values.
Results may differ from a plain program's by a relative error of at most 0.0003.
Values may be sent and summed in bfloat16 or wider, within the bound.
A program may use at most 64 MiB of HBM per device.

v0:
```python
import jax
import jax.numpy as jnp
from jax import lax
from jax.sharding import PartitionSpec as P

CRE_LOC = 2048
TILE = 128
BLOCK = 128
ITERS = 2
NEG_FILL = -1e30
TAU_INV = 4.0
STEP_RATE = 0.5


def block_table(block_lists, block_counts, local_blocks, cre_index):
    block_ids = cre_index * local_blocks + lax.iota(jnp.int32, local_blocks)
    in_list = lax.iota(jnp.int32, block_lists.shape[1])[None, :] < block_counts[:, None]
    matches = (block_lists[:, :, None] == block_ids[None, None, :]) & in_list[:, :, None]
    allowed = jnp.any(matches, axis=1)
    allowed = jnp.repeat(allowed, TILE, axis=0)
    return jnp.repeat(allowed, BLOCK, axis=1)


def scored(impressions, panel_rows, price_rows, col_mask):
    affinity = lax.dot_general(
        impressions, panel_rows, (((1,), (1,)), ((), ())), preferred_element_type=jnp.float32
    )
    logit_vals = TAU_INV * affinity + price_rows[None, :]
    return jnp.where(col_mask, logit_vals, NEG_FILL)


def sweep(panel_rows, group_prices, mask_full, running, update):
    col_count = panel_rows.shape[0]
    sub_width = 512

    def inner(current, step_index):
        shift_cols = step_index * sub_width
        part_panel = lax.dynamic_slice_in_dim(panel_rows, shift_cols, sub_width, 0)
        part_price = lax.dynamic_slice_in_dim(group_prices, shift_cols, sub_width, 0)
        part_mask = lax.dynamic_slice_in_dim(mask_full, shift_cols, sub_width, 1)
        return (update(current, part_panel, part_price, part_mask, shift_cols), None)

    current, _ = lax.scan(inner, running, jnp.arange(col_count // sub_width, dtype=jnp.int32))
    return current


def shards(impressions, panels, block_lists, block_counts, imp_weight, spend_goals, prices):
    local_blocks = CRE_LOC // BLOCK
    mask_full = block_table(block_lists, block_counts, local_blocks, lax.axis_index("cre"))
    imp_rows = impressions.shape[0]
    owned_rows = prices.shape[1]
    owned_start = lax.axis_index("imp") * owned_rows

    def max_step(current, panel_rows, price_rows, col_mask, first_col):
        row_top, row_total = current
        masked = scored(impressions, panel_rows, price_rows, col_mask)
        block_top = jnp.max(masked, axis=1)
        new_top = jnp.maximum(row_top, block_top)
        block_sum = jnp.sum(jnp.where(col_mask, jnp.exp(masked - block_top[:, None]), 0.0), axis=1)
        return (
            new_top,
            row_total * jnp.exp(row_top - new_top) + block_sum * jnp.exp(block_top - new_top),
        )

    spend_owned = None
    row_norm = None
    for iteration in range(ITERS):
        start_state = (
            jnp.full((imp_rows,), NEG_FILL, jnp.float32),
            jnp.zeros((imp_rows,), jnp.float32),
        )
        empty_spend = jnp.zeros((CRE_LOC,), jnp.float32)
        whole_prices = lax.all_gather(prices, "imp", axis=1, tiled=True)[0]
        row_top, row_total = sweep(
            lax.all_gather(panels, "imp", axis=1, tiled=True)[0],
            whole_prices,
            mask_full,
            start_state,
            max_step,
        )
        merged_top = lax.pmax(row_top, "cre")
        row_total = lax.psum(row_total * jnp.exp(row_top - merged_top), "cre")
        row_top = merged_top
        row_norm = row_top + jnp.log(row_total)

        def spend_step(current, panel_rows, price_rows, col_mask, first_col):
            masked = scored(impressions, panel_rows, price_rows, col_mask)
            shares = jnp.where(col_mask, jnp.exp(masked - row_norm[:, None]), 0.0)
            col_spend = jnp.sum(imp_weight[:, None] * shares, axis=0)
            return lax.dynamic_update_slice_in_dim(current, col_spend, first_col, 0)

        partial_spend = sweep(
            lax.all_gather(panels, "imp", axis=1, tiled=True)[0],
            whole_prices,
            mask_full,
            empty_spend,
            spend_step,
        )
        summed = lax.psum(partial_spend, "imp")
        spend_owned = lax.dynamic_slice_in_dim(summed, owned_start, owned_rows, 0)
        spend_owned = spend_owned.reshape(1, owned_rows)
        prices = prices + STEP_RATE * (
            jnp.log(spend_goals) - jnp.log(spend_owned + 0.25 * spend_goals)
        )
    return (prices, spend_owned, row_norm)


def solution(mesh):
    placed = (
        P("imp", None),
        P("cre", "imp", None),
        P("imp", None),
        P("imp"),
        P("imp"),
        P("cre", "imp"),
        P("cre", "imp"),
    )
    return jax.shard_map(
        shards,
        mesh=mesh,
        in_specs=placed,
        out_specs=(P("cre", "imp"), P("cre", "imp"), P("imp")),
        check_vma=False,
    )
```

profile of v0, /device:TPU:1, one launch (start us, length us, event | category | flops | bytes accessed | tf_op | source)
XLA Modules:
  0.0 427.9 jit_solution(15510092804575440473)
XLA Ops:
  7.2 0.7 all-gather.2.cloned.1.call-update
  8.0 0.7 iota_compare_fusion
  8.7 0.8 and_reduce_fusion
  9.7 1.3 dynamic-slice
  11.6 0.8 bitcast_dynamic-update-slice_fusion.1
  12.4 70.3 %all-reduce = f32[2048]{0:T(1024)S(1)} all-reduce(f32[2048]{0:T(1024)S(1)} %bitcast_dynamic-update-slice_fusion.1), channel_id=1, replica_groups=mesh['imp'=32,'cre'=8] {'imp'}, use_global_device_ids=true, to_apply=%add | all-reduce | flops 2048 | bytes 16384 | tf_op jit(solution)/shard_map/squeeze | solution.py:73
  82.8 9.8 %all-gather.2.cloned.1.call-done = bf16[1,2048,256]{2,1,0:T(8,128)(2,1)} async-done(((bf16[1,64,256]{2,1,0:T(8,128)(2,1)}), bf16[1,2048,256]{2,1,0:T(8,128)(2,1)}) %all-gather.2.cloned.1.call-update) | async-done | bytes 1048592 | tf_op jit(solution)/shard_map/all_gather | solution.py:93
  92.5 0.5 broadcast_in_dim.47
  93.1 0.7 copy-done.3
  93.7 15.7 %while.48 = (s32[]{:T(128)}, f32[1024]{0:T(1024)S(1)}, f32[1024]{0:T(1024)S(1)}, s32[4]{0:T(128)S(1)}, pred[1024,2048]{0,1:T(32,128)(4,1)S(1)}, /*index=5*/bf16[...) while((s32[]{:T(128)}, f32[1024]{0:T(1024)S(1)}, ...), condition=%wide.region_4.5_spmd.clone, body=%wide.region_1.4_spmd.clone.sunk | while | flops 273684480 | bytes 6075585 | solution.py:43
  93.8 0.7 dynamic_slice.118
  95.2 1.7 fusion.49
  96.9 0.8 select_reduce_fusion.4
  97.7 0.7 dynamic_slice.118
  99.1 1.7 fusion.49
  100.8 0.8 select_reduce_fusion.4
  101.6 0.7 dynamic_slice.118
  103.0 1.7 fusion.49
  104.7 0.8 select_reduce_fusion.4
  105.5 0.7 dynamic_slice.118
  107.0 1.7 fusion.49
  108.6 0.8 select_reduce_fusion.4
  109.4 14.9 %pmax.14 = f32[1024]{0:T(1024)S(1)} all-reduce(f32[1024]{0:T(1024)S(1)} %get-tuple-element.183), channel_id=1, replica_groups=mesh['imp'=32,'cre'=8] {'cre'}, use_global_device_ids=true, to_apply=%region_5.6 | all-reduce | flops 1024 | bytes 8192 | tf_op jit(solution)/shard_map/pmax | solution.py:81
  124.4 12.5 %psum.28 = f32[1024]{0:T(1024)S(1)} all-reduce(f32[1024]{0:T(1024)S(1)} %exponential_multiply_fusion.1), channel_id=1, replica_groups=mesh['imp'=32,'cre'=8] {'cre'}, use_global_device_ids=true, to_apply=%region_6.7 | all-reduce | flops 1024 | bytes 8192 | tf_op jit(solution)/shard_map/psum | solution.py:82
  136.9 14.6 %while.46 = (s32[]{:T(128)}, f32[2048]{0:T(1024)S(1)}, f32[1024]{0:T(1024)S(1)}, s32[4]{0:T(128)S(1)}, pred[1024,2048]{0,1:T(32,128)(4,1)S(1)}, /*index=5*/bf16[...) while((s32[]{:T(128)}, f32[2048]{0:T(1024)S(1)}, ...), condition=%wide.region_9.10_spmd, body=%wide.region_7.9_spmd.sunk | while | flops 272104960 | bytes 1332415 | solution.py:43
  136.9 0.6 dynamic_slice.109
  138.2 2.1 fusion.44
  140.3 0.3 dynamic_update_slice.8
  140.6 0.6 dynamic_slice.109
  141.9 2.1 fusion.44
  144.0 0.3 dynamic_update_slice.8
  144.2 0.6 dynamic_slice.109
  145.6 2.1 fusion.44
  147.9 0.6 dynamic_slice.109
  149.2 2.1 fusion.44
  151.5 72.9 %psum.29 = f32[2048]{0:T(1024)S(1)} all-reduce(f32[2048]{0:T(1024)S(1)} %get-tuple-element.185), channel_id=1, replica_groups=mesh['imp'=32,'cre'=8] {'imp'}, use_global_device_ids=true, to_apply=%region_10.11 | all-reduce | flops 2048 | bytes 16384 | tf_op jit(solution)/shard_map/psum | solution.py:99
  224.6 66.0 %all-reduce.1 = f32[2048]{0:T(1024)S(1)} all-reduce(f32[2048]{0:T(1024)S(1)} %get-tuple-element.317), channel_id=1, replica_groups=mesh['imp'=32,'cre'=8] {'imp'}, use_global_device_ids=true, to_apply=%add.1 | all-reduce | flops 2048 | bytes 16384 | tf_op jit(solution)/shard_map/squeeze | solution.py:73
  290.7 15.2 %while.49 = (s32[]{:T(128)}, f32[1024]{0:T(1024)S(1)}, f32[1024]{0:T(1024)S(1)}, s32[4]{0:T(128)S(1)}, pred[1024,2048]{0,1:T(32,128)(4,1)S(1)}, /*index=5*/bf16[...) while((s32[]{:T(128)}, f32[1024]{0:T(1024)S(1)}, ...), condition=%wide.region_14.15_spmd.clone, body=%wide.region_11.14_spmd.clone.sunk | while | flops 273684480 | bytes 6075585 | solution.py:43
  290.7 0.6 dynamic_slice.123
  292.0 1.7 fusion.52
  293.7 0.8 select_reduce_fusion.5
  294.5 0.6 dynamic_slice.123
  295.8 1.7 fusion.52
  297.5 0.8 select_reduce_fusion.5
  298.3 0.6 dynamic_slice.123
  299.6 1.7 fusion.52
  301.3 0.8 select_reduce_fusion.5
  302.1 0.6 dynamic_slice.123
  303.4 1.7 fusion.52
  305.1 0.8 select_reduce_fusion.5
  305.9 14.2 %pmax.15 = f32[1024]{0:T(1024)S(1)} all-reduce(f32[1024]{0:T(1024)S(1)} %get-tuple-element.186), channel_id=1, replica_groups=mesh['imp'=32,'cre'=8] {'cre'}, use_global_device_ids=true, to_apply=%region_15.16 | all-reduce | flops 1024 | bytes 8192 | tf_op jit(solution)/shard_map/pmax | solution.py:81
  320.0 12.8 %psum.30 = f32[1024]{0:T(1024)S(1)} all-reduce(f32[1024]{0:T(1024)S(1)} %exponential_multiply_fusion), channel_id=1, replica_groups=mesh['imp'=32,'cre'=8] {'cre'}, use_global_device_ids=true, to_apply=%region_16.17 | all-reduce | flops 1024 | bytes 8192 | tf_op jit(solution)/shard_map/psum | solution.py:82
  332.8 14.6 %while.47 = (s32[]{:T(128)}, f32[2048]{0:T(1024)S(1)}, f32[1024]{0:T(1024)S(1)}, s32[4]{0:T(128)S(1)}, pred[1024,2048]{0,1:T(32,128)(4,1)S(1)}, /*index=5*/bf16[...) while((s32[]{:T(128)}, f32[2048]{0:T(1024)S(1)}, ...), condition=%wide.region_19.20_spmd, body=%wide.region_17.19_spmd.sunk | while | flops 272104960 | bytes 1332415 | solution.py:43
  332.8 0.6 dynamic_slice.113
  334.1 2.1 fusion.47
  336.2 0.3 dynamic_update_slice.9
  336.5 0.6 dynamic_slice.113
  337.8 2.1 fusion.47
  340.2 0.6 dynamic_slice.113
  341.5 2.1 fusion.47
  343.8 0.6 dynamic_slice.113
  345.1 2.1 fusion.47
  347.4 73.0 %psum.31 = f32[2048]{0:T(1024)S(1)} all-reduce(f32[2048]{0:T(1024)S(1)} %get-tuple-element.188), channel_id=1, replica_groups=mesh['imp'=32,'cre'=8] {'imp'}, use_global_device_ids=true, to_apply=%region_20.21 | all-reduce | flops 2048 | bytes 16384 | tf_op jit(solution)/shard_map/psum | solution.py:99
  420.5 0.6 multiply_add_fusion
  (60 shorter events, 3.1 us)
Async XLA Ops:
  7.2 85.4 %all-gather.2.cloned.1.call-start = ((), (), s32[]{:S(2)}) async-start(), calls=%async_computation | async-start | bytes 1081344 | tf_op jit(solution)/shard_map/all_gather | solution.py:93
  92.5 1.2 copy-start.3
  93.7 43.1 %copy-start.4 = (f32[1024]{0:T(1024)S(1)}, f32[1024]{0:T(1024)}, u32[]{:S(2)}) copy-start(f32[1024]{0:T(1024)} %param.19) | copy-start | bytes 12292
  136.9 87.5 %copy-start.1 = (f32[1,64]{1,0:T(1,128)S(1)}, f32[1,64]{1,0:T(1,128)}, u32[]{:S(2)}) copy-start(f32[1,64]{1,0:T(1,128)} %param.20) | copy-start | bytes 772
  136.9 87.5 %copy-start.2 = (f32[1,64]{1,0:T(1,128)S(1)}, f32[1,64]{1,0:T(1,128)}, u32[]{:S(2)}) copy-start(f32[1,64]{1,0:T(1,128)} %param.21) | copy-start | bytes 772
  347.4 73.7 %copy-start = (f32[1024]{0:T(1024)}, f32[1024]{0:T(1024)S(1)}, u32[]{:S(2)}) copy-start(f32[1024]{0:T(1024)S(1)} %get-tuple-element.705) | copy-start | bytes 12292
Sparse Core Ops, SparseCore 0:
  10.8 81.6 all-gather.1
where the time goes:
time: 429 us; the launch traced here: 428 us
  blocking collectives  337 us (79%)
  matrix products  29.8 us (7%)
  local copies, waits for them, and re-layouts  16.5 us (4%)
  between operations  14.9 us (3%)
  loops' own time  11 us (3%)
  waiting for transfers between devices  10.4 us (2%)
  other arithmetic  8.58 us (2%)
    psum x2, blocking collectives, shards(): summed = lax.psum(partial_spend, 'imp')  146 us
    squeeze x2, blocking collectives, shards(): whole_prices = lax.all_gather(prices, 'imp', axis=1, tiled=True)[0]  136 us
    dot_general x16, matrix products, scored(): lax.dot_general(impressions, panel_rows, (((1,), (1,)), ((), ())), prefer...  29.8 us
    pmax x2, blocking collectives, shards(): merged_top = lax.pmax(row_top, 'cre')  29.1 us
    psum x2, blocking collectives, shards(): row_total = lax.psum(row_total * jnp.exp(row_top - merged_top), 'cre')  25.2 us
    another operation x4, loops' own time, sweep(): lax.scan(inner, running, jnp.arange(col_count // sub_width, dtype=jnp.int...  11 us
    all_gather x1, waiting for transfers between devices, shards(): lax.all_gather(panels, 'imp', axis=1, tiled=True)[0]  9.76 us
    dynamic_slice x16, local copies, waits for them, and re-layouts, sweep(): lax.scan(inner, running, jnp.arange(col_count // sub_width, dtype=jnp.int...  9.67 us
  transfers between devices with their start and end apart: 1, of which 1 were waited for; matrix products, arithmetic and copies ran while one was open for 1% of the time, Pallas kernels for 0%

commit v1 on v0

--- a/solution.py
+++ b/solution.py
@@ -90,7 +90,9 @@
             return lax.dynamic_update_slice_in_dim(current, col_spend, first_col, 0)
 
         partial_spend = sweep(
-            lax.all_gather(panels, "imp", axis=1, tiled=True)[0],
+            jnp.concatenate(
+                lax.all_to_all(jnp.stack([panels] * lax.axis_size("imp")), "imp", 0, 0), axis=1
+            )[0],
             whole_prices,
             mask_full,
             empty_spend,

time: 429 us -> 445 us (1.037)
  blocking collectives: 337 us -> 350 us
  starting transfers between devices: 0.04 us -> 12.8 us
  waiting for transfers between devices: 10.4 us -> 0.7 us
    squeeze x2, blocking collectives: 136 us -> 150 us  [shards(): whole_prices = lax.all_gather(prices, 'imp', axis=1, tiled=True)[0]]
    all_to_all x0 -> x1, starting transfers between devices: none -> 12.8 us  [shards(): lax.all_to_all(jnp.stack([panels] * lax.axis_size('imp')), 'imp', 0, 0)]
    all_gather x1, waiting for transfers between devices: 9.76 us -> 0.02 us  [shards(): lax.all_gather(panels, 'imp', axis=1, tiled=True)[0]]
  transfers between devices with their start and end apart: 1 -> 2, of which waited for: 1 -> 0; matrix products, arithmetic and copies ran while one was open for 1% -> 4% of each run, Pallas kernels for 0% -> 0%
where the time goes in v1:
time: 445 us; the launch traced here: 443 us
  blocking collectives  350 us (79%)
  matrix products  30.5 us (7%)
  local copies, waits for them, and re-layouts  16.2 us (4%)
  between operations  15 us (3%)
  starting transfers between devices  12.8 us (3%)
  loops' own time  10.8 us (2%)
  other arithmetic  7.22 us (2%)
    squeeze x2, blocking collectives, shards(): whole_prices = lax.all_gather(prices, 'imp', axis=1, tiled=True)[0]  150 us
    psum x2, blocking collectives, shards(): summed = lax.psum(partial_spend, 'imp')  146 us
    dot_general x16, matrix products, scored(): lax.dot_general(impressions, panel_rows, (((1,), (1,)), ((), ())), prefer...  30.5 us
    pmax x2, blocking collectives, shards(): merged_top = lax.pmax(row_top, 'cre')  29.3 us
    psum x2, blocking collectives, shards(): row_total = lax.psum(row_total * jnp.exp(row_top - merged_top), 'cre')  25.2 us
    all_to_all x1, starting transfers between devices, shards(): lax.all_to_all(jnp.stack([panels] * lax.axis_size('imp')), 'imp', 0, 0)  12.8 us
    another operation x4, loops' own time, sweep(): lax.scan(inner, running, jnp.arange(col_count // sub_width, dtype=jnp.int...  10.8 us
    dynamic_slice x16, local copies, waits for them, and re-layouts, sweep(): lax.scan(inner, running, jnp.arange(col_count // sub_width, dtype=jnp.int...  9.39 us
  transfers between devices with their start and end apart: 2, of which 0 were waited for; matrix products, arithmetic and copies ran while one was open for 4% of the time, Pallas kernels for 0%

profile of v1, /device:TPU:1, one launch (start us, length us, event | category | flops | bytes accessed | tf_op | source)
XLA Modules:
  0.0 443.0 jit_solution(8327474467549978428)
XLA Ops:
  7.3 0.7 all-gather.2.cloned.1.call-update
  7.9 1.9 stack.2
  9.9 12.8 %all-to-all-start = ((bf16[32,1,64,256]{3,2,1,0:T(8,128)(2,1)}), bf16[32,1,64,256]{3,2,1,0:T(8,128)(2,1)S(1)}, u32[]{:S(2)}, u32[]{:S(2)}) async-start(bf16[32,1,64,256]{3,2,1,0:T(8,128)(2,1)} %stack.2), calls=%async_computation | async-start | bytes 2097152 | tf_op jit(solution)/shard_map/all_to_all | solution.py:94
  23.1 0.6 dynamic-slice
  24.5 83.6 %all-reduce = f32[2048]{0:T(1024)S(1)} all-reduce(f32[2048]{0:T(1024)S(1)} %bitcast_dynamic-update-slice_fusion.1), channel_id=1, replica_groups=mesh['imp'=32,'cre'=8] {'imp'}, use_global_device_ids=true, to_apply=%add | all-reduce | flops 2048 | bytes 16384 | tf_op jit(solution)/shard_map/squeeze | solution.py:73
  108.1 0.5 broadcast_in_dim.47
  108.7 15.4 %while.48 = (s32[]{:T(128)}, f32[1024]{0:T(1024)S(1)}, f32[1024]{0:T(1024)S(1)}, s32[4]{0:T(128)S(1)}, pred[1024,2048]{0,1:T(32,128)(4,1)S(1)}, /*index=5*/bf16[...) while((s32[]{:T(128)}, f32[1024]{0:T(1024)S(1)}, ...), condition=%wide.region_4.5_spmd.clone, body=%wide.region_1.4_spmd.clone.sunk | while | flops 273684480 | bytes 6075585 | solution.py:43
  108.7 0.6 dynamic_slice.118
  110.0 1.7 fusion.49
  111.7 0.8 select_reduce_fusion.4
  112.5 0.6 dynamic_slice.118
  113.8 1.7 fusion.49
  115.6 0.8 select_reduce_fusion.4
  116.4 0.6 dynamic_slice.118
  117.7 1.7 fusion.49
  119.5 0.8 select_reduce_fusion.4
  120.3 0.6 dynamic_slice.118
  121.6 1.7 fusion.49
  123.3 0.8 select_reduce_fusion.4
  124.1 15.1 %pmax.14 = f32[1024]{0:T(1024)S(1)} all-reduce(f32[1024]{0:T(1024)S(1)} %get-tuple-element.183), channel_id=1, replica_groups=mesh['imp'=32,'cre'=8] {'cre'}, use_global_device_ids=true, to_apply=%region_5.6 | all-reduce | flops 1024 | bytes 8192 | tf_op jit(solution)/shard_map/pmax | solution.py:81
  139.2 12.5 %psum.28 = f32[1024]{0:T(1024)S(1)} all-reduce(f32[1024]{0:T(1024)S(1)} %exponential_multiply_fusion.1), channel_id=1, replica_groups=mesh['imp'=32,'cre'=8] {'cre'}, use_global_device_ids=true, to_apply=%region_6.7 | all-reduce | flops 1024 | bytes 8192 | tf_op jit(solution)/shard_map/psum | solution.py:82
  151.7 14.6 %while.46 = (s32[]{:T(128)}, f32[2048]{0:T(1024)S(1)}, f32[1024]{0:T(1024)S(1)}, s32[4]{0:T(128)S(1)}, pred[1024,2048]{0,1:T(32,128)(4,1)S(1)}, /*index=5*/bf16[...) while((s32[]{:T(128)}, f32[2048]{0:T(1024)S(1)}, ...), condition=%wide.region_9.10_spmd, body=%wide.region_7.9_spmd.sunk | while | flops 272104960 | bytes 1332415 | solution.py:43
  151.7 0.6 dynamic_slice.109
  153.0 2.1 fusion.44
  155.1 0.3 dynamic_update_slice.8
  155.4 0.6 dynamic_slice.109
  156.7 2.1 fusion.44
  158.8 0.3 dynamic_update_slice.8
  159.1 0.6 dynamic_slice.109
  160.4 2.1 fusion.44
  162.5 0.3 dynamic_update_slice.8
  162.7 0.6 dynamic_slice.109
  164.0 2.1 fusion.44
  166.1 0.3 dynamic_update_slice.8
  166.3 72.7 %psum.29 = f32[2048]{0:T(1024)S(1)} all-reduce(f32[2048]{0:T(1024)S(1)} %get-tuple-element.185), channel_id=1, replica_groups=mesh['imp'=32,'cre'=8] {'imp'}, use_global_device_ids=true, to_apply=%region_10.11 | all-reduce | flops 2048 | bytes 16384 | tf_op jit(solution)/shard_map/psum | solution.py:101
  239.3 66.0 %all-reduce.1 = f32[2048]{0:T(1024)S(1)} all-reduce(f32[2048]{0:T(1024)S(1)} %get-tuple-element.317), channel_id=1, replica_groups=mesh['imp'=32,'cre'=8] {'imp'}, use_global_device_ids=true, to_apply=%add.1 | all-reduce | flops 2048 | bytes 16384 | tf_op jit(solution)/shard_map/squeeze | solution.py:73
  305.4 15.5 %while.49 = (s32[]{:T(128)}, f32[1024]{0:T(1024)S(1)}, f32[1024]{0:T(1024)S(1)}, s32[4]{0:T(128)S(1)}, pred[1024,2048]{0,1:T(32,128)(4,1)S(1)}, /*index=5*/bf16[...) while((s32[]{:T(128)}, f32[1024]{0:T(1024)S(1)}, ...), condition=%wide.region_14.15_spmd.clone, body=%wide.region_11.14_spmd.clone.sunk | while | flops 273684480 | bytes 6075585 | solution.py:43
  305.4 0.6 dynamic_slice.123
  306.7 1.7 fusion.52
  308.4 0.8 select_reduce_fusion.5
  309.2 0.6 dynamic_slice.123
  310.6 1.7 fusion.52
  312.3 0.8 select_reduce_fusion.5
  313.1 0.6 dynamic_slice.123
  314.5 1.7 fusion.52
  316.2 0.8 select_reduce_fusion.5
  317.0 0.6 dynamic_slice.123
  318.3 1.7 fusion.52
  320.1 0.8 select_reduce_fusion.5
  320.9 14.2 %pmax.15 = f32[1024]{0:T(1024)S(1)} all-reduce(f32[1024]{0:T(1024)S(1)} %get-tuple-element.186), channel_id=1, replica_groups=mesh['imp'=32,'cre'=8] {'cre'}, use_global_device_ids=true, to_apply=%region_15.16 | all-reduce | flops 1024 | bytes 8192 | tf_op jit(solution)/shard_map/pmax | solution.py:81
  335.1 12.7 %psum.30 = f32[1024]{0:T(1024)S(1)} all-reduce(f32[1024]{0:T(1024)S(1)} %exponential_multiply_fusion), channel_id=1, replica_groups=mesh['imp'=32,'cre'=8] {'cre'}, use_global_device_ids=true, to_apply=%region_16.17 | all-reduce | flops 1024 | bytes 8192 | tf_op jit(solution)/shard_map/psum | solution.py:82
  347.9 14.6 %while.47 = (s32[]{:T(128)}, f32[2048]{0:T(1024)S(1)}, f32[1024]{0:T(1024)S(1)}, s32[4]{0:T(128)S(1)}, pred[1024,2048]{0,1:T(32,128)(4,1)S(1)}, /*index=5*/bf16[...) while((s32[]{:T(128)}, f32[2048]{0:T(1024)S(1)}, ...), condition=%wide.region_19.20_spmd, body=%wide.region_17.19_spmd.sunk | while | flops 272104960 | bytes 1332415 | solution.py:43
  347.9 0.6 dynamic_slice.113
  349.2 2.1 fusion.47
  351.3 0.3 dynamic_update_slice.9
  351.5 0.6 dynamic_slice.113
  352.9 2.1 fusion.47
  354.9 0.3 dynamic_update_slice.9
  355.2 0.6 dynamic_slice.113
  356.5 2.1 fusion.47
  358.8 0.6 dynamic_slice.113
  360.2 2.1 fusion.47
  362.5 73.0 %psum.31 = f32[2048]{0:T(1024)S(1)} all-reduce(f32[2048]{0:T(1024)S(1)} %get-tuple-element.188), channel_id=1, replica_groups=mesh['imp'=32,'cre'=8] {'imp'}, use_global_device_ids=true, to_apply=%region_20.21 | all-reduce | flops 2048 | bytes 16384 | tf_op jit(solution)/shard_map/psum | solution.py:101
  435.5 0.6 multiply_add_fusion
  (67 shorter events, 2.7 us)
Async XLA Ops:
  7.2 15.9 %copy-start.6 = (u32[256]{0:T(256)S(1)}, u32[256]{0:T(256)}, u32[]{:S(2)}) copy-start(u32[256]{0:T(256)} %constant.107) | copy-start | bytes 3076
  7.2 15.5 %copy-start.5 = (s32[8]{0:T(128)S(1)}, s32[8]{0:T(128)}, u32[]{:S(2)}) copy-start(s32[8]{0:T(128)} %param.18) | copy-start | bytes 100
  7.2 15.6 %copy-start.1 = (s32[8,16]{1,0:T(8,128)S(1)}, s32[8,16]{1,0:T(8,128)}, u32[]{:S(2)}) copy-start(s32[8,16]{1,0:T(8,128)} %param.17) | copy-start | bytes 1540
  7.2 17.2 %copy-start.3 = (f32[1,64]{1,0:T(1,128)S(1)}, f32[1,64]{1,0:T(1,128)}, u32[]{:S(2)}) copy-start(f32[1,64]{1,0:T(1,128)} %param.21) | copy-start | bytes 772
  7.2 100.9 %all-gather.2.cloned.1.call-start = ((), (), s32[]{:S(2)}) async-start(), calls=%async_computation.1 | async-start | bytes 1081344 | tf_op jit(solution)/shard_map/all_gather | solution.py:75
  9.9 141.8 %all-to-all-start = ((bf16[32,1,64,256]{3,2,1,0:T(8,128)(2,1)}), bf16[32,1,64,256]{3,2,1,0:T(8,128)(2,1)S(1)}, u32[]{:S(2)}, u32[]{:S(2)}) async-start(bf16[32,1,64,256]{3,2,1,0:T(8,128)(2,1)} %stack.2), calls=%async_computation | async-start | bytes 2097152 | tf_op jit(solution)/shard_map/all_to_all | solution.py:94
  108.7 43.0 %copy-start.4 = (f32[1024]{0:T(1024)S(1)}, f32[1024]{0:T(1024)}, u32[]{:S(2)}) copy-start(f32[1024]{0:T(1024)} %param.19) | copy-start | bytes 12292
  151.7 87.4 %copy-start.2 = (f32[1,64]{1,0:T(1,128)S(1)}, f32[1,64]{1,0:T(1,128)}, u32[]{:S(2)}) copy-start(f32[1,64]{1,0:T(1,128)} %param.20) | copy-start | bytes 772
  362.5 73.6 %copy-start = (f32[1024]{0:T(1024)}, f32[1024]{0:T(1024)S(1)}, u32[]{:S(2)}) copy-start(f32[1024]{0:T(1024)S(1)} %get-tuple-element.707) | copy-start | bytes 12292
Sparse Core Ops, SparseCore 0:
  10.8 84.2 all-gather.1
